TPU v7x, 32 devices: a whole 2x2x4 slice. The times are simulated.
32 devices in a mesh: adapter: 8 (over z, x), feature: 4 (over y, core).
Axes of the slice: x: 2, y: 2, z: 4, core: 2. Of those that a mesh axis runs over, the one named last changes fastest.
Arguments:
- adapter_down: bfloat16 [128, 16, 8192], P('adapter', None, 'feature'), may hold values from -6 to 6
- adapter_up: bfloat16 [128, 16, 8192], P('adapter', None, 'feature'), may hold values from -6 to 6
- fisher: float32 [128], P('adapter'), may hold values from 0.1 to 10
- init_v: float32 [8192, 64], P('feature'), may hold values from -0.0625 to 0.0625
- init_u: float32 [8192, 64], P('feature'), may hold values from -0.0625 to 0.0625
- prompt_rows: bfloat16 [4096, 8192], P('adapter', 'feature'), may hold values from -6 to 6
- request_ids: int32 [32], P('adapter'), may hold values from 0 to 127
Outputs:
- served: bfloat16 [4096, 8192], P('adapter', 'feature')
All inputs are finite; a program needn't handle non-finite values.
Results may differ from a plain program's by a relative error of at most 0.025.
Values may be sent and summed in bfloat16 or wider, within the bound.
A program may use at most 64 MiB of HBM per device.

v0:
```python
import functools

import jax
import jax.numpy as jnp
from jax import lax
from jax.experimental import pallas as pl
from jax.experimental.pallas import tpu as pltpu
from jax.sharding import PartitionSpec as P

SWEEPS = 3
GROUP = 8


highest = lax.Precision.HIGHEST


def dot32(left, right):
    return jnp.dot(left, right, precision=highest, preferred_element_type=jnp.float32)


def dot_nt(left, right):
    return lax.dot_general(
        left, right, (((1,), (1,)), ((), ())), preferred_element_type=jnp.float32
    )


def inverse_factor(gram):
    width = gram.shape[0]
    rows = lax.broadcasted_iota(jnp.int32, (width, width), 0)
    columns = lax.broadcasted_iota(jnp.int32, (width, width), 1)
    eye = (rows == columns).astype(jnp.float32)
    table = jnp.concatenate([gram, eye], axis=1)
    blocks = [table[at : at + GROUP] for at in range(0, width, GROUP)]
    inner = lax.broadcasted_iota(jnp.int32, (GROUP, 1), 0)
    for k in range(width):
        first, offset = divmod(k, GROUP)
        row = blocks[first][offset : offset + 1]
        scaled = row / row[:, k : k + 1]
        for b in range(first, len(blocks)):
            factor = blocks[b][:, k : k + 1]
            if b == first:
                factor = jnp.where(inner > offset, factor, 0.0)
            blocks[b] = blocks[b] - factor * scaled
    table = jnp.concatenate(blocks, axis=0)
    pivots = jnp.sum(table[:, :width] * eye, axis=1, keepdims=True)
    return table[:, width:] / jnp.sqrt(pivots)


def weigh(rank, fresh, other, weights):
    total = fresh.shape[1]
    step = 128 if total % 128 == 0 and 128 % rank == 0 else total
    same = (
        lax.broadcasted_iota(jnp.int32, (step, step), 0) // rank
        == lax.broadcasted_iota(jnp.int32, (step, step), 1) // rank
    )
    parts = []
    for at in range(0, total, step):
        piece = fresh[:, at : at + step]
        inner = jnp.where(same, dot32(piece.T, piece), 0.0)
        parts.append(dot32(other[:, at : at + step], inner))
    joined = parts[0] if len(parts) == 1 else jnp.concatenate(parts, axis=1)
    return (joined * weights).astype(jnp.bfloat16)


def first_kernel(rank, fresh_ref, other_ref, weights_ref, flat_ref, term_ref):
    low = weigh(rank, fresh_ref[...], other_ref[...], weights_ref[...])
    term_ref[...] = jnp.dot(low, flat_ref[...], preferred_element_type=jnp.float32)


def turn_kernel(rank, sums_ref, other_ref, weights_ref, flat_ref, inverse_ref, fresh_ref, term_ref):
    extent = fresh_ref.shape[1]
    inverse = inverse_factor(sums_ref[:, extent:])
    inverse_ref[...] = inverse
    fresh = dot32(inverse, sums_ref[:, :extent])
    fresh_ref[...] = fresh
    low = weigh(rank, fresh, other_ref[...], weights_ref[...])
    term_ref[...] = jnp.dot(low, flat_ref[...], preferred_element_type=jnp.float32)


def last_kernel(sums_ref, fresh_ref):
    extent = fresh_ref.shape[1]
    inverse = inverse_factor(sums_ref[:, extent:])
    fresh_ref[...] = dot32(inverse, sums_ref[:, :extent])


def gram_kernel(full_ref, *refs):
    full = full_ref[...]
    high = full.astype(jnp.bfloat16)
    low = (full - high.astype(jnp.float32)).astype(jnp.bfloat16)
    both = jnp.concatenate([high, low], axis=0)
    width = full.shape[0]
    *stacks, sums_ref = refs
    at = 0
    for stack in stacks:
        pair = dot_nt(both, stack[...])
        sums_ref[:, at : at + pair.shape[1]] = pair[:width] + pair[width:]
        at += pair.shape[1]
    quad = dot_nt(both, both)
    half = quad[:width] + quad[width:]
    sums_ref[:, at : at + width] = half[:, :width] + half[:, width:]


def call(body, shapes, *args):
    return pl.pallas_call(
        body,
        out_shape=[jax.ShapeDtypeStruct(shape, jnp.float32) for shape in shapes],
        compiler_params=pltpu.CompilerParams(vmem_limit_bytes=40 * 2**20),
    )(*args)


def on_device(adapter_down, adapter_up, fisher, init_v, init_u, prompt_rows, request_ids):
    count_local, rank, depth = adapter_up.shape
    width = init_v.shape[1]
    rows = count_local * rank
    down = adapter_down.reshape(rows, depth)
    up = adapter_up.reshape(rows, depth)
    weights = jnp.repeat(fisher, rank)[None, :]

    def start(basis, flat):
        return lax.dot_general(
            basis.astype(jnp.bfloat16),
            flat,
            (((0,), (1,)), ((), ())),
            preferred_element_type=jnp.float32,
        )

    def sums(full, *stacks):
        extent = sum(stack.shape[0] for stack in stacks)
        (partial,) = call(gram_kernel, [(width, extent + width)], full, *stacks)
        return lax.psum(partial, "feature")

    both = lax.psum(
        jnp.concatenate([start(init_v, down), start(init_u, up)], axis=1), "feature"
    )
    rows_p, cols_q = both[:, :rows], both[:, rows:]
    shape_term, shape_rows, shape_gram = (width, depth), (width, rows), (width, width)
    (term,) = call(
        functools.partial(first_kernel, rank), [shape_term], rows_p, cols_q, weights, up
    )
    turn = functools.partial(turn_kernel, rank)
    shapes = [shape_gram, shape_rows, shape_term]
    for sweep_index in range(SWEEPS):
        full_u = lax.psum(term, "adapter")
        total = sums(full_u, up)
        inverse_u, cols_q, term = call(turn, shapes, total, rows_p, weights, down)
        full_v = lax.psum(term, "adapter")
        if sweep_index < SWEEPS - 1:
            total = sums(full_v, down)
            _, rows_p, term = call(turn, shapes, total, cols_q, weights, up)
    total = sums(full_v, down, prompt_rows)
    (fresh,) = call(last_kernel, [(width, rows + prompt_rows.shape[0])], total)
    rows_p, hidden = fresh[:, :rows], fresh[:, rows:].astype(jnp.bfloat16)
    basis_u = dot32(inverse_u, full_u).astype(jnp.bfloat16)
    final_cores = jnp.einsum(
        "kir,lir->ikl",
        cols_q.reshape(width, count_local, rank),
        rows_p.reshape(width, count_local, rank),
        precision=highest,
    ).astype(jnp.bfloat16)
    flat_cores = final_cores.reshape(count_local, width * width)
    every_core = lax.all_gather(flat_cores, "adapter", axis=0, tiled=True)
    onehot = (
        request_ids[:, None] == jnp.arange(every_core.shape[0], dtype=jnp.int32)[None, :]
    ).astype(jnp.bfloat16)
    own_cores = jnp.dot(onehot, every_core, preferred_element_type=jnp.float32).astype(jnp.bfloat16)
    blocks = own_cores.shape[0]
    mixed = jnp.einsum(
        "lbn,bkl->bnk",
        hidden.reshape(width, blocks, -1),
        own_cores.reshape(blocks, width, width),
        preferred_element_type=jnp.float32,
    ).astype(jnp.bfloat16)
    served = jnp.dot(
        mixed.reshape(-1, width), basis_u, preferred_element_type=jnp.float32
    )
    return served.astype(jnp.bfloat16)


def solution(mesh):
    placed = (
        P("adapter", None, "feature"),
        P("adapter", None, "feature"),
        P("adapter"),
        P("feature", None),
        P("feature", None),
        P("adapter", "feature"),
        P("adapter"),
    )
    return jax.shard_map(
        on_device, mesh=mesh, in_specs=placed, out_specs=P("adapter", "feature"), check_vma=False
    )
```

profile of v0, /device:TPU:0, one launch (start us, length us, event | category | flops | bytes accessed | tf_op | source)
XLA Modules:
  0.0 790.3 jit_solution(9633796602967134183)
XLA Ops:
  6.5 1.9 fusion.3
  8.5 1.8 fusion.1
  10.3 0.7 pad_maximum_fusion
  11.0 0.0 all-reduce.16.cloned.1.call-start
  11.1 0.1 broadcast_in_dim.2
  11.1 0.1 broadcast_in_dim_reshape.3.weights_ref
  11.2 34.5 %all-reduce.14.cloned.1.call-done = f32[64,512]{1,0:T(8,128)} async-done(((f32[64,512]{1,0:T(8,128)}), f32[64,512]{1,0:T(8,128)}) %all-reduce.14.cloned.1.call-update) | async-done | bytes 131088 | tf_op jit(solution)/shard_map/psum | solution.py:132
  45.7 0.9 fusion.11
  46.6 1.7 shard_map.73
  48.3 73.6 %all-reduce.16.cloned.1.call-done.full_ref = f32[64,2048]{1,0:T(8,128)} async-done(((f32[64,2048]{1,0:T(8,128)}), f32[64,2048]{1,0:T(8,128)}) %all-reduce.16.cloned.1.call-update) | async-done | bytes 524304 | tf_op jit(solution)/shard_map/psum | solution.py:143
  121.9 1.0 copy-done.5
  122.9 1.3 shard_map.74
  124.3 31.0 %all-reduce.18.cloned.1.call-done.sums_ref = f32[64,320]{1,0:T(8,128)} async-done(((f32[64,320]{1,0:T(8,128)}), f32[64,320]{1,0:T(8,128)}) %all-reduce.18.cloned.1.call-update) | async-done | bytes 81936 | tf_op jit(solution)/shard_map/psum | solution.py:130
  155.3 0.9 copy-done.15
  156.2 7.4 shard_map.75
  163.6 0.0 all-reduce.22.cloned.1.call-start
  163.7 72.8 %all-reduce.20.cloned.1.call-done.full_ref = f32[64,2048]{1,0:T(8,128)} async-done(((f32[64,2048]{1,0:T(8,128)}), f32[64,2048]{1,0:T(8,128)}) %all-reduce.20.cloned.1.call-update) | async-done | bytes 524304 | tf_op jit(solution)/shard_map/psum | solution.py:146
  236.4 1.0 copy-done.6
  237.5 1.3 shard_map.76
  238.8 0.0 all-reduce.24.cloned.1.call-start
  238.8 31.0 %all-reduce.22.cloned.1.call-done.sums_ref = f32[64,320]{1,0:T(8,128)} async-done(((f32[64,320]{1,0:T(8,128)}), f32[64,320]{1,0:T(8,128)}) %all-reduce.22.cloned.1.call-update) | async-done | bytes 81936 | tf_op jit(solution)/shard_map/psum | solution.py:130
  269.8 0.9 copy-done.12
  270.7 7.4 shard_map.77
  278.2 72.8 %all-reduce.24.cloned.1.call-done.full_ref = f32[64,2048]{1,0:T(8,128)} async-done(((f32[64,2048]{1,0:T(8,128)}), f32[64,2048]{1,0:T(8,128)}) %all-reduce.24.cloned.1.call-update) | async-done | bytes 524304 | tf_op jit(solution)/shard_map/psum | solution.py:143
  350.9 1.0 copy-done.7
  351.9 1.3 shard_map.78
  353.3 0.0 all-reduce.28.cloned.1.call-start
  353.3 31.0 %all-reduce.26.cloned.1.call-done.sums_ref = f32[64,320]{1,0:T(8,128)} async-done(((f32[64,320]{1,0:T(8,128)}), f32[64,320]{1,0:T(8,128)}) %all-reduce.26.cloned.1.call-update) | async-done | bytes 81936 | tf_op jit(solution)/shard_map/psum | solution.py:130
  384.3 0.9 copy-done.13
  385.2 7.4 shard_map.79
  392.7 72.8 %all-reduce.28.cloned.1.call-done.full_ref = f32[64,2048]{1,0:T(8,128)} async-done(((f32[64,2048]{1,0:T(8,128)}), f32[64,2048]{1,0:T(8,128)}) %all-reduce.28.cloned.1.call-update) | async-done | bytes 524304 | tf_op jit(solution)/shard_map/psum | solution.py:146
  465.4 1.0 copy-done.8
  466.5 1.3 shard_map.80
  467.8 0.0 all-reduce.32.cloned.1.call-start
  467.8 31.0 %all-reduce.30.cloned.1.call-done.sums_ref = f32[64,320]{1,0:T(8,128)} async-done(((f32[64,320]{1,0:T(8,128)}), f32[64,320]{1,0:T(8,128)}) %all-reduce.30.cloned.1.call-update) | async-done | bytes 81936 | tf_op jit(solution)/shard_map/psum | solution.py:130
  498.8 0.9 copy-done.14
  499.7 7.4 shard_map.81
  507.1 0.0 all-reduce.34.cloned.1.call-start
  507.2 72.8 %all-reduce.32.cloned.1.call-done.full_ref = f32[64,2048]{1,0:T(8,128)} async-done(((f32[64,2048]{1,0:T(8,128)}), f32[64,2048]{1,0:T(8,128)}) %all-reduce.32.cloned.1.call-update) | async-done | bytes 524304 | tf_op jit(solution)/shard_map/psum | solution.py:143
  579.9 1.0 copy-done.2
  581.0 1.3 shard_map.82
  582.3 0.2 all-reduce.36.cloned.1.call-start
  582.5 30.8 %all-reduce.34.cloned.1.call-done.sums_ref = f32[64,320]{1,0:T(8,128)} async-done(((f32[64,320]{1,0:T(8,128)}), f32[64,320]{1,0:T(8,128)}) %all-reduce.34.cloned.1.call-update) | async-done | bytes 81936 | tf_op jit(solution)/shard_map/psum | solution.py:130
  613.3 0.9 copy-done.11
  614.2 7.4 shard_map.83
  621.6 0.0 all-reduce.38.cloned.1.call-start
  621.7 72.7 %all-reduce.36.cloned.1.call-done.full_ref = f32[64,2048]{1,0:T(8,128)} async-done(((f32[64,2048]{1,0:T(8,128)}), f32[64,2048]{1,0:T(8,128)}) %all-reduce.36.cloned.1.call-update) | async-done | bytes 524304 | tf_op jit(solution)/shard_map/psum | solution.py:146
  694.4 1.6 copy-done.4
  696.0 1.0 copy-done.9
  697.1 2.0 shard_map.84
  699.1 0.0 all-gather.2.cloned.1.call-start
  699.2 0.1 copy.11
  699.3 31.4 %all-reduce.38.cloned.1.call-done.sums_ref = f32[64,832]{1,0:T(8,128)} async-done(((f32[64,832]{1,0:T(8,128)}), f32[64,832]{1,0:T(8,128)}) %all-reduce.38.cloned.1.call-update) | async-done | bytes 213008 | tf_op jit(solution)/shard_map/psum | solution.py:130
  730.6 0.9 copy-done.10
  731.6 5.8 shard_map.85
  737.4 0.1 copy.12
  737.5 1.0 convolution_convert_fusion.3
  738.5 0.9 reshape.30
  739.5 0.6 convolution_convert_fusion.2
  740.1 39.8 %all-gather.2.cloned.1.call-done = bf16[128,4096]{1,0:T(8,128)(2,1)} async-done(((bf16[16,4096]{1,0:T(8,128)(2,1)}), bf16[128,4096]{1,0:T(8,128)(2,1)}) %all-gather.2.cloned.1.call-update) | async-done | bytes 1048592 | tf_op jit(solution)/shard_map/all_gather | solution.py:161
  779.9 1.5 convolution_convert_fusion
  781.5 0.1 reshape.31
  781.6 0.1 fusion
  781.7 2.1 convolution_convert_fusion.1
  (43 shorter events, 0.4 us)
Async XLA Ops:
  6.5 40.0 %copy-start = (bf16[16,16,2048]{2,1,0:T(8,128)(2,1)S(1)}, bf16[16,16,2048]{2,1,0:T(8,128)(2,1)}, u32[]{:S(2)}) copy-start(bf16[16,16,2048]{2,1,0:T(8,128)(2,1)} %param.8) | copy-start | bytes 3145732
  6.5 4.5 copy-start.17
  6.5 39.1 %all-reduce.14.cloned.1.call-start = ((), (), s32[]{:S(2)}) async-start(), calls=%async_computation | async-start | bytes 262144 | tf_op jit(solution)/shard_map/psum | solution.py:132
  11.0 110.9 %all-reduce.16.cloned.1.call-start = ((), (), s32[]{:S(2)}) async-start(), calls=%async_computation.1 | async-start | bytes 1048576 | tf_op jit(solution)/shard_map/psum | solution.py:143
  11.2 144.1 %copy-start.1 = (bf16[16,16,2048]{2,1,0:T(8,128)(2,1)S(1)}, bf16[16,16,2048]{2,1,0:T(8,128)(2,1)}, u32[]{:S(2)}) copy-start(bf16[16,16,2048]{2,1,0:T(8,128)(2,1)} %param.7) | copy-start | bytes 3145732
  48.2 107.0 %all-reduce.18.cloned.1.call-start = ((), (), s32[]{:S(2)}) async-start(), calls=%async_computation.2 | async-start | bytes 196608 | tf_op jit(solution)/shard_map/psum | solution.py:130
  121.9 1.0 copy-start.5
  124.3 112.1 %all-reduce.20.cloned.1.call-start = ((), (), s32[]{:S(2)}) async-start(), calls=%async_computation.3 | async-start | bytes 1048576 | tf_op jit(solution)/shard_map/psum | solution.py:146
  155.3 0.9 copy-start.15
  163.6 106.2 %all-reduce.22.cloned.1.call-start = ((), (), s32[]{:S(2)}) async-start(), calls=%async_computation.4 | async-start | bytes 196608 | tf_op jit(solution)/shard_map/psum | solution.py:130
  236.4 1.0 copy-start.6
  238.8 112.1 %all-reduce.24.cloned.1.call-start = ((), (), s32[]{:S(2)}) async-start(), calls=%async_computation.5 | async-start | bytes 1048576 | tf_op jit(solution)/shard_map/psum | solution.py:143
  269.8 0.9 copy-start.12
  278.1 106.2 %all-reduce.26.cloned.1.call-start = ((), (), s32[]{:S(2)}) async-start(), calls=%async_computation.6 | async-start | bytes 196608 | tf_op jit(solution)/shard_map/psum | solution.py:130
  350.9 1.0 copy-start.7
  353.3 112.1 %all-reduce.28.cloned.1.call-start = ((), (), s32[]{:S(2)}) async-start(), calls=%async_computation.7 | async-start | bytes 1048576 | tf_op jit(solution)/shard_map/psum | solution.py:146
  384.3 0.9 copy-start.13
  392.6 106.2 %all-reduce.30.cloned.1.call-start = ((), (), s32[]{:S(2)}) async-start(), calls=%async_computation.8 | async-start | bytes 196608 | tf_op jit(solution)/shard_map/psum | solution.py:130
  465.4 1.0 copy-start.8
  467.8 112.1 %all-reduce.32.cloned.1.call-start = ((), (), s32[]{:S(2)}) async-start(), calls=%async_computation.9 | async-start | bytes 1048576 | tf_op jit(solution)/shard_map/psum | solution.py:143
  498.8 0.9 copy-start.14
  507.1 106.2 %all-reduce.34.cloned.1.call-start = ((), (), s32[]{:S(2)}) async-start(), calls=%async_computation.10 | async-start | bytes 196608 | tf_op jit(solution)/shard_map/psum | solution.py:130
  579.9 1.0 copy-start.2
  582.3 112.1 %all-reduce.36.cloned.1.call-start = ((), (), s32[]{:S(2)}) async-start(), calls=%async_computation.11 | async-start | bytes 1048576 | tf_op jit(solution)/shard_map/psum | solution.py:146
  613.3 0.9 copy-start.11
  621.6 117.9 %copy-start.3 = (f32[64,2048]{1,0:T(8,128)S(1)}, f32[64,2048]{1,0:T(8,128)}, u32[]{:S(2)}) copy-start(f32[64,2048]{1,0:T(8,128)} %all-reduce.32.cloned.1.call-done.full_ref) | copy-start | bytes 1572868
  621.6 109.0 %all-reduce.38.cloned.1.call-start = ((), (), s32[]{:S(2)}) async-start(), calls=%async_computation.12 | async-start | bytes 458752 | tf_op jit(solution)/shard_map/psum | solution.py:130
  694.4 1.6 copy-start.4
  696.0 1.0 copy-start.9
  699.1 80.8 %copy-start.16 = (s32[4]{0:T(128)S(1)}, s32[4]{0:T(128)}, u32[]{:S(2)}) copy-start(s32[4]{0:T(128)} %param.13) | copy-start | bytes 52
  699.1 80.8 %all-gather.2.cloned.1.call-start = ((), (), s32[]{:S(2)}) async-start(), calls=%async_computation.13 | async-start | bytes 1179648 | tf_op jit(solution)/shard_map/all_gather | solution.py:161
  730.6 0.9 copy-start.10
Sparse Core Ops, SparseCore 0:
  11.1 34.5 all-reduce.13
  49.1 72.7 all-reduce.15
  124.4 30.8 all-reduce.17
  163.7 72.6 all-reduce.19
  238.9 30.8 all-reduce.21
  278.2 72.6 all-reduce.23
  353.4 30.8 all-reduce.25
  392.7 72.6 all-reduce.27
  467.9 30.8 all-reduce.29
  507.2 72.6 all-reduce.31
  582.4 30.8 all-reduce.33
  621.7 72.6 all-reduce.35
  699.2 31.3 all-reduce.37
  739.6 40.2 all-gather.1
where the time goes:
time: 791 us; the launch traced here: 790 us
  waiting for transfers between devices  698 us (88%)
  Pallas kernels  53.1 us (7%)
  local copies, waits for them, and re-layouts  15.5 us (2%)
  between operations  13.4 us (2%)
  matrix products  9.07 us (1%)
    psum x3, waiting for transfers between devices, on_device(): full_u = lax.psum(term, 'adapter')  219 us
    psum x3, waiting for transfers between devices, on_device(): full_v = lax.psum(term, 'adapter')  218 us
    psum x6, waiting for transfers between devices, sums(): return lax.psum(partial, 'feature')  186 us
    pallas_call x13, Pallas kernels, call(): pl.pallas_call(body, out_shape=[jax.ShapeDtypeStruct(shape, jnp.float32)...  53.1 us
    all_gather x1, waiting for transfers between devices, on_device(): every_core = lax.all_gather(flat_cores, 'adapter', axis=0, tiled=True)  39.8 us
    psum x1, waiting for transfers between devices, on_device(): lax.psum(jnp.concatenate([start(init_v, down), start(init_u, up)], axis=1...  34.5 us
  transfers between devices with their start and end apart: 14, of which 14 were waited for; matrix products, arithmetic and copies ran while one was open for 0% of the time, Pallas kernels for 0%

commit v1 on v0

v1 whole, which is shorter than its diff:
```python
import functools
import math

import jax
import jax.numpy as jnp
from jax import lax
from jax.experimental import pallas as pl
from jax.experimental.pallas import tpu as pltpu
from jax.sharding import PartitionSpec as P

SWEEPS = 3
GROUP = 8
LANES = 128
MESH = pl.DeviceIdType.MESH
SEND = jnp.bfloat16

highest = lax.Precision.HIGHEST


def dot32(left, right):
    return jnp.dot(left, right, precision=highest, preferred_element_type=jnp.float32)


def dot_nt(left, right):
    return lax.dot_general(
        left, right, (((1,), (1,)), ((), ())), preferred_element_type=jnp.float32
    )


def inverse_factor(gram):
    width = gram.shape[0]
    rows = lax.broadcasted_iota(jnp.int32, (width, width), 0)
    columns = lax.broadcasted_iota(jnp.int32, (width, width), 1)
    eye = (rows == columns).astype(jnp.float32)
    table = jnp.concatenate([gram, eye], axis=1)
    blocks = [table[at : at + GROUP] for at in range(0, width, GROUP)]
    inner = lax.broadcasted_iota(jnp.int32, (GROUP, 1), 0)
    for k in range(width):
        first, offset = divmod(k, GROUP)
        row = blocks[first][offset : offset + 1]
        scaled = row / row[:, k : k + 1]
        for b in range(first, len(blocks)):
            factor = blocks[b][:, k : k + 1]
            if b == first:
                factor = jnp.where(inner > offset, factor, 0.0)
            blocks[b] = blocks[b] - factor * scaled
    table = jnp.concatenate(blocks, axis=0)
    pivots = jnp.sum(table[:, :width] * eye, axis=1, keepdims=True)
    return table[:, width:] / jnp.sqrt(pivots)


def weigh(rank, fresh, other, weights):
    total = fresh.shape[1]
    step = 128 if total % 128 == 0 and 128 % rank == 0 else total
    same = (
        lax.broadcasted_iota(jnp.int32, (step, step), 0) // rank
        == lax.broadcasted_iota(jnp.int32, (step, step), 1) // rank
    )
    parts = []
    for at in range(0, total, step):
        piece = fresh[:, at : at + step]
        inner = jnp.where(same, dot32(piece.T, piece), 0.0)
        parts.append(dot32(other[:, at : at + step], inner))
    joined = parts[0] if len(parts) == 1 else jnp.concatenate(parts, axis=1)
    return (joined * weights).astype(jnp.bfloat16)


def fold(square):
    half = square.shape[0] // 2
    return jnp.concatenate([square[:half], square[half:]], axis=1)


def unfold(packed):
    width = packed.shape[1] // 2
    return jnp.concatenate([packed[:, :width], packed[:, width:]], axis=0)


def kernel(
    na,
    nf,
    rank,
    down_ref,
    up_ref,
    prompt_ref,
    init_v_ref,
    init_u_ref,
    weights_ref,
    ids_ref,
    mixed_ref,
    basis_ref,
    flat,
    prompt,
    factors,
    part,
    arrived,
    numerator,
    proj_out,
    gram_out,
    proj_in,
    gram_in,
    init_out,
    init_in,
    hidden_out,
    hidden_in,
    all_q,
    all_p,
    load_sem,
    prompt_sem,
    scatter_sem,
    gather_sem,
    proj_sem,
    gram_sem,
    init_sem,
    hidden_sem,
    q_sem,
    p_sem,
):
    a = lax.axis_index("adapter")
    f = lax.axis_index("feature")
    _, count, rows, chunk = flat.shape
    width = part.shape[1]
    mine = lax.rem(a, count)
    base = a - mine
    far = [lax.rem(a + r, na) for r in range(1, na)]
    group = [base + lax.rem(mine + r, count) for r in range(1, count)]
    beside = [lax.rem(f + r, nf) for r in range(1, nf)]

    loads = []
    for w, ref in enumerate((down_ref, up_ref)):
        for c in range(count):
            loads.append(
                pltpu.make_async_copy(
                    ref.at[:, pl.ds(c * chunk, chunk)], flat.at[w, c], load_sem.at[w, c]
                )
            )
    prompt_loads = [
        pltpu.make_async_copy(
            prompt_ref.at[:, pl.ds(c * chunk, chunk)], prompt.at[c], prompt_sem.at[c]
        )
        for c in range(count)
    ]
    for copy in loads + prompt_loads:
        copy.start()

    barrier = pltpu.get_barrier_semaphore()
    for to in far:
        pl.semaphore_signal(barrier, inc=1, device_id=(to, f), device_id_type=MESH)
    for to in beside:
        pl.semaphore_signal(barrier, inc=1, device_id=(a, to), device_id_type=MESH)

    def over_adapter(source, target, sems, r, to):
        return pltpu.make_async_remote_copy(
            src_ref=source,
            dst_ref=target,
            send_sem=sems.at[0, r],
            recv_sem=sems.at[1, r],
            device_id=(to, f),
            device_id_type=MESH,
        )

    def over_feature(source, target, sems, r, to):
        return pltpu.make_async_remote_copy(
            src_ref=source,
            dst_ref=target,
            send_sem=sems.at[0, r],
            recv_sem=sems.at[1, r],
            device_id=(a, to),
            device_id_type=MESH,
        )

    for w, ref in enumerate((init_v_ref, init_u_ref)):
        total = jnp.zeros((rows, width), jnp.float32)
        for c in range(count):
            loads[w * count + c].wait()
            basis = ref[c * chunk : (c + 1) * chunk, :].astype(jnp.bfloat16)
            total += jnp.dot(flat[w, c], basis, preferred_element_type=jnp.float32)
        init_out[w] = total.T.astype(init_out.dtype)
    pl.semaphore_wait(barrier, na - 1 + nf - 1)
    copies = [
        over_feature(init_out, init_in.at[r], init_sem, r, to) for r, to in enumerate(beside)
    ]
    for copy in copies:
        copy.start()
    for copy in copies:
        copy.wait()
    total = init_out[...].astype(jnp.float32)
    for r in range(nf - 1):
        total += init_in[r].astype(jnp.float32)
    factors[...] = total

    weights = weights_ref[...]

    def half(h, last):
        even = 1 - lax.rem(h, 2)
        w = even
        parity = 1 - even
        low = weigh(rank, factors[1 - w], factors[w], weights)
        for c in range(count):
            part[c] = jnp.dot(low, flat[w, c], preferred_element_type=jnp.float32).astype(part.dtype)
        scatter = [
            over_adapter(part.at[lax.rem(to, count)], arrived.at[r], scatter_sem, r, to)
            for r, to in enumerate(far)
        ]
        for copy in scatter:
            copy.start()
        total = part[mine].astype(jnp.float32)
        for r, copy in enumerate(scatter):
            copy.wait_recv()
            total += arrived[r].astype(jnp.float32)
        own = total.astype(numerator.dtype)
        numerator[parity, mine] = own
        gather = [
            over_adapter(numerator.at[parity, mine], numerator.at[parity, mine], gather_sem, r, to)
            for r, to in enumerate(group)
        ]
        for copy in gather:
            copy.start()
        proj = dot_nt(own, flat[w, mine])
        gram = dot_nt(own, own)
        if last:
            hidden = dot_nt(own, prompt[mine])
        for r, copy in enumerate(gather):
            copy.wait_recv()
            c = lax.rem(mine + (count - 1 - r), count)
            piece = numerator[parity, c]
            proj += dot_nt(piece, flat[w, c])
            gram += dot_nt(piece, piece)
            if last:
                hidden += dot_nt(piece, prompt[c])
        proj_out[...] = proj.astype(proj_out.dtype)
        gram_out[...] = fold(gram)
        sends = []
        for r, to in enumerate(beside):
            sends.append(
                over_feature(gram_out, gram_in.at[parity, r], gram_sem.at[parity], r, to)
            )
        for r, to in enumerate(beside):
            sends.append(
                over_feature(proj_out, proj_in.at[parity, r], proj_sem.at[parity], r, to)
            )
        for copy in sends:
            copy.start()
        if last:
            hidden_out[...] = hidden.astype(hidden_out.dtype)
            late = [
                over_feature(hidden_out, hidden_in.at[r], hidden_sem, r, to)
                for r, to in enumerate(beside)
            ]
            for copy in late:
                copy.start()
        for copy in sends[: nf - 1]:
            copy.wait_recv()
        square = gram_out[...]
        for r in range(nf - 1):
            square += gram_in[parity, r]
        inverse = inverse_factor(unfold(square))
        for copy in sends[nf - 1 :]:
            copy.wait_recv()
        total = proj_out[...].astype(jnp.float32)
        for r in range(nf - 1):
            total += proj_in[parity, r].astype(jnp.float32)
        fresh = dot32(inverse, total)
        factors[w] = fresh
        for copy in scatter + gather + sends:
            copy.wait_send()
        if not last:
            return inverse
        return inverse, fresh, late

    inverse_u = lax.fori_loop(
        0,
        2 * SWEEPS - 1,
        lambda h, _: half(h, False),
        jnp.zeros((width, width), jnp.float32),
    )
    all_q[a] = factors[1].astype(all_q.dtype)
    spread_q = [over_adapter(all_q.at[a], all_q.at[a], q_sem, r, to) for r, to in enumerate(far)]
    for copy in spread_q:
        copy.start()
    for c in range(count):
        basis_ref[:, c * chunk : (c + 1) * chunk] = dot32(
            inverse_u, numerator[0, c].astype(jnp.float32)
        ).astype(basis_ref.dtype)
    for copy in prompt_loads:
        copy.wait()
    inverse_v, fresh, late = half(2 * SWEEPS - 1, True)
    all_p[a] = fresh.astype(all_p.dtype)
    spread_p = [over_adapter(all_p.at[a], all_p.at[a], p_sem, r, to) for r, to in enumerate(far)]
    for copy in spread_p:
        copy.start()
    for copy in late:
        copy.wait()
    total = hidden_out[...].astype(jnp.float32)
    for r in range(nf - 1):
        total += hidden_in[r].astype(jnp.float32)
    hidden = dot32(inverse_v, total).astype(jnp.bfloat16)
    for copy in spread_q + spread_p:
        copy.wait()
    blocks = ids_ref.shape[0]
    block = hidden.shape[1] // blocks
    owner = lax.broadcasted_iota(jnp.int32, (1, rows), 1) // rank
    for b in range(blocks):
        at = ids_ref[b]
        device, inside = at // (rows // rank), lax.rem(at, rows // rank)
        chosen_q = jnp.where(owner == inside, all_q[device], 0)
        core = dot_nt(chosen_q, all_p[device]).astype(jnp.bfloat16)
        mixed = jnp.dot(
            core, hidden[:, b * block : (b + 1) * block], preferred_element_type=jnp.float32
        )
        mixed_ref[b * block : (b + 1) * block, :] = mixed.T.astype(mixed_ref.dtype)


def on_device(na, nf, adapter_down, adapter_up, fisher, init_v, init_u, prompt_rows, request_ids):
    count_local, rank, depth = adapter_up.shape
    width = init_v.shape[1]
    rows = count_local * rank
    down = adapter_down.reshape(rows, depth)
    up = adapter_up.reshape(rows, depth)
    weights = jnp.repeat(fisher, rank)[None, :]
    tall = prompt_rows.shape[0]
    count = math.gcd(na, depth // LANES)
    chunk = depth // count
    dma = pltpu.SemaphoreType.DMA
    anywhere = pl.BlockSpec(memory_space=pl.ANY)
    vmem = pl.BlockSpec(memory_space=pltpu.VMEM)
    mixed, basis_u = pl.pallas_call(
        functools.partial(kernel, na, nf, rank),
        out_shape=[
            jax.ShapeDtypeStruct((tall, width), jnp.bfloat16),
            jax.ShapeDtypeStruct((width, depth), jnp.bfloat16),
        ],
        in_specs=[anywhere] * 3 + [vmem] * 3 + [pl.BlockSpec(memory_space=pltpu.SMEM)],
        out_specs=[vmem, vmem],
        scratch_shapes=[
            pltpu.VMEM((2, count, rows, chunk), jnp.bfloat16),
            pltpu.VMEM((count, tall, chunk), jnp.bfloat16),
            pltpu.VMEM((2, width, rows), jnp.float32),
            pltpu.VMEM((count, width, chunk), SEND),
            pltpu.VMEM((na - 1, width, chunk), SEND),
            pltpu.VMEM((2, count, width, chunk), jnp.bfloat16),
            pltpu.VMEM((width, rows), SEND),
            pltpu.VMEM((width // 2, 2 * width), jnp.float32),
            pltpu.VMEM((2, nf - 1, width, rows), SEND),
            pltpu.VMEM((2, nf - 1, width // 2, 2 * width), jnp.float32),
            pltpu.VMEM((2, width, rows), SEND),
            pltpu.VMEM((nf - 1, 2, width, rows), SEND),
            pltpu.VMEM((width, tall), SEND),
            pltpu.VMEM((nf - 1, width, tall), SEND),
            pltpu.VMEM((na, width, rows), jnp.bfloat16),
            pltpu.VMEM((na, width, rows), jnp.bfloat16),
            dma((2, count)),
            dma((count,)),
            dma((2, na - 1)),
            dma((2, count - 1)),
            dma((2, 2, nf - 1)),
            dma((2, 2, nf - 1)),
            dma((2, nf - 1)),
            dma((2, nf - 1)),
            dma((2, na - 1)),
            dma((2, na - 1)),
        ],
        compiler_params=pltpu.CompilerParams(
            vmem_limit_bytes=48 * 2**20, collective_id=0, has_side_effects=True
        ),
    )(down, up, prompt_rows, init_v, init_u, weights, request_ids)
    served = jnp.dot(mixed, basis_u, preferred_element_type=jnp.float32)
    return served.astype(jnp.bfloat16)


def solution(mesh):
    placed = (
        P("adapter", None, "feature"),
        P("adapter", None, "feature"),
        P("adapter"),
        P("feature", None),
        P("feature", None),
        P("adapter", "feature"),
        P("adapter"),
    )
    body = functools.partial(on_device, mesh.shape["adapter"], mesh.shape["feature"])
    return jax.shard_map(
        body, mesh=mesh, in_specs=placed, out_specs=P("adapter", "feature"), check_vma=False
    )
```

time: 791 us -> 178 us (0.23)
  waiting for transfers between devices: 698 us -> 0 us
  Pallas kernels: 53.1 us -> 171 us
  between operations: 13.4 us -> 0.05 us
  local copies, waits for them, and re-layouts: 15.5 us -> 4.87 us
    psum x13 -> x0, waiting for transfers between devices: 658 us -> none  [the longest x3 219 us: on_device(): full_u = lax.psum(term, 'adapter')]
    pallas_call x13 -> x1, Pallas kernels: 53.1 us -> 171 us  [on_device(): pl.pallas_call(functools.partial(kernel, na, nf, rank), out_shape=[jax.Sh...]
    all_gather x1 -> x0, waiting for transfers between devices: 39.8 us -> none  [on_device(): every_core = lax.all_gather(flat_cores, 'adapter', axis=0, tiled=True)]
    unnamed x36 -> x8, local copies, waits for them, and re-layouts: 13.3 us -> 3.97 us
  transfers between devices with their start and end apart: 14 -> 0, of which waited for: 14 -> 0; matrix products, arithmetic and copies ran while one was open for 0% -> 0% of each run, Pallas kernels for 0% -> 0%
where the time goes in v1:
time: 178 us
  Pallas kernels  171 us (96%)
  local copies, waits for them, and re-layouts  4.87 us (3%)
  matrix products  2 us (1%)
    pallas_call x1, Pallas kernels, on_device(): pl.pallas_call(functools.partial(kernel, na, nf, rank), out_shape=[jax.Sh...  171 us
    unnamed x8, local copies, waits for them, and re-layouts  3.97 us

profile of v1, /device:TPU:0, one launch (start us, length us, event | category | flops | bytes accessed | tf_op | source)
XLA Modules:
  0.0 177.6 jit_solution(5306657631004949270)
XLA Ops:
  0.0 0.0 copy-start.2
  0.0 0.0 copy-start
  0.0 0.8 broadcast_in_dim.3
  0.8 0.1 broadcast_in_dim_reshape.3.weights_ref
  0.9 1.4 copy.8.init_v_ref
  2.3 1.4 copy.9.init_u_ref
  3.7 0.0 copy-done.2
  3.7 0.0 copy-done
  3.7 0.0 copy-start.1
  3.7 1.2 copy-done.1
  4.9 170.6 %shard_map.73 = (bf16[512,64]{1,0:T(8,128)(2,1)S(1)}, bf16[64,2048]{1,0:T(8,128)(2,1)S(1)}) custom-call(bf16[256,2048]{1,0:T(8,128)(2,1)S(1)} %bitcast.4, bf16[256,2048]{1,0:T(8,128)(2,1)S(1)} %bitcast.5, bf16[512,2048]{1,0:T(8,128)(2,1)} %prompt_ref.1, f32[2048,64]{1,0:T(8,128)S(1)} %copy.8.init_v_ref, f32[2048,64]{1,0:T(8,128)S(1)} %copy.9.init_u_ref, ...), custom_call_target="tpu_custom_call" | custom-call | tf_op jit(solution)/shard_map/pallas_call | solution.py:326
  175.6 2.0 %convolution_convert_fusion = bf16[512,2048]{1,0:T(8,128)(2,1)} fusion(bf16[512,64]{1,0:T(8,128)(2,1)S(1)} %get-tuple-element.7, bf16[64,2048]{1,0:T(8,128)(2,1)S(1)} %get-tuple-element.8), kind=kOutput, calls=%fused_computation | convolution fusion | flops 135266304 | bytes 2424832 | tf_op jit(solution)/shard_map/dot_general | solution.py:366
Async XLA Ops:
  0.0 3.7 %copy-start.2 = (s32[4]{0:T(128)S(1)}, s32[4]{0:T(128)}, u32[]{:S(2)}) copy-start(s32[4]{0:T(128)} %ids_ref.1) | copy-start | bytes 52
  0.0 3.7 %copy-start = (bf16[16,16,2048]{2,1,0:T(8,128)(2,1)S(1)}, bf16[16,16,2048]{2,1,0:T(8,128)(2,1)}, u32[]{:S(2)}) copy-start(bf16[16,16,2048]{2,1,0:T(8,128)(2,1)} %param.7) | copy-start | bytes 3145732
  3.7 1.2 copy-start.1

commit v2 on v1

v2 whole, which is shorter than its diff:
```python
import functools
import math

import jax
import jax.numpy as jnp
from jax import lax
from jax.experimental import pallas as pl
from jax.experimental.pallas import tpu as pltpu
from jax.sharding import PartitionSpec as P

SWEEPS = 3
GROUP = 8
LANES = 128
MESH = pl.DeviceIdType.MESH
SUBS = 2
SEND = jnp.bfloat16

highest = lax.Precision.HIGHEST


def dot32(left, right):
    return jnp.dot(left, right, precision=highest, preferred_element_type=jnp.float32)


def dot_nt(left, right):
    return lax.dot_general(
        left, right, (((1,), (1,)), ((), ())), preferred_element_type=jnp.float32
    )


def dot_split(left, right):
    left_high, right_high = left.astype(jnp.bfloat16), right.astype(jnp.bfloat16)
    left_low = (left - left_high.astype(jnp.float32)).astype(jnp.bfloat16)
    right_low = (right - right_high.astype(jnp.float32)).astype(jnp.bfloat16)
    dot = functools.partial(jnp.dot, preferred_element_type=jnp.float32)
    return dot(left_high, right_high) + (dot(left_high, right_low) + dot(left_low, right_high))


def inverse_factor(gram):
    width = gram.shape[0]
    shape = (width, width)
    eye = lax.broadcasted_iota(jnp.int32, shape, 0) == lax.broadcasted_iota(jnp.int32, shape, 1)
    table = jnp.concatenate([gram, eye.astype(jnp.float32)], axis=1)
    blocks = [table[at : at + GROUP] for at in range(0, width, GROUP)]
    full = functools.partial(jnp.broadcast_to, shape=(GROUP, 2 * width))
    inner = lax.broadcasted_iota(jnp.int32, (GROUP, 2 * width), 0)
    result = []
    for b, block in enumerate(blocks):
        at = b * GROUP
        columns = [full(block[:, at + j : at + j + 1]) for j in range(GROUP)]
        entry = [[full(columns[j][i : i + 1]) for j in range(i + 1)] for i in range(GROUP)]
        row = [full(block[i : i + 1]) for i in range(GROUP)]
        inverse = []
        done = None
        for i in range(GROUP):
            inverse.append(1.0 / entry[i][i])
            for j in range(i + 1, GROUP):
                factor = entry[j][i] * inverse[i]
                for q in range(i + 1, j + 1):
                    entry[j][q] = entry[j][q] - factor * entry[q][i]
                row[j] = row[j] - factor * row[i]
            scaled = row[i] / jnp.sqrt(entry[i][i])
            done = scaled if done is None else jnp.where(inner == i, scaled, done)
        result.append(done)
        for c in range(b + 1, len(blocks)):
            columns = [full(blocks[c][:, at + j : at + j + 1]) for j in range(GROUP)]
            new = blocks[c]
            for i in range(GROUP):
                factor = columns[i] * inverse[i]
                for j in range(i + 1, GROUP):
                    columns[j] = columns[j] - factor * entry[j][i]
                new = new - factor * row[i]
            blocks[c] = new
    return jnp.concatenate(result, axis=0)[:, width:]


def weigh(rank, fresh, other, weights):
    total = fresh.shape[1]
    step = 128 if total % 128 == 0 and 128 % rank == 0 else total
    same = (
        lax.broadcasted_iota(jnp.int32, (step, step), 0) // rank
        == lax.broadcasted_iota(jnp.int32, (step, step), 1) // rank
    )
    parts = []
    for at in range(0, total, step):
        piece = fresh[:, at : at + step]
        inner = jnp.where(same, dot_split(piece.T, piece), 0.0)
        parts.append(dot_split(other[:, at : at + step], inner))
    joined = parts[0] if len(parts) == 1 else jnp.concatenate(parts, axis=1)
    return (joined * weights).astype(jnp.bfloat16)


def fold(square):
    half = square.shape[0] // 2
    return jnp.concatenate([square[:half], square[half:]], axis=1)


def unfold(packed):
    width = packed.shape[1] // 2
    return jnp.concatenate([packed[:, :width], packed[:, width:]], axis=0)


def kernel(
    na,
    nf,
    rank,
    down_ref,
    up_ref,
    prompt_ref,
    init_v_ref,
    init_u_ref,
    weights_ref,
    ids_ref,
    mixed_ref,
    basis_ref,
    flat,
    prompt,
    factors,
    part,
    arrived,
    numerator,
    proj_out,
    gram_out,
    proj_in,
    gram_in,
    init_out,
    init_in,
    hidden_out,
    hidden_in,
    all_q,
    all_p,
    inverse_ref,
    load_sem,
    prompt_sem,
    scatter_sem,
    gather_sem,
    proj_sem,
    gram_sem,
    init_sem,
    hidden_sem,
    q_sem,
    p_sem,
):
    a = lax.axis_index("adapter")
    f = lax.axis_index("feature")
    _, count, rows, chunk = flat.shape
    _, subs, width, sub = part.shape
    mine = lax.rem(a, count)
    base = a - mine
    far = [lax.rem(a + r, na) for r in range(1, na)]
    beside = [lax.rem(f + r, nf) for r in range(1, nf)]

    loads = []
    for w, ref in enumerate((down_ref, up_ref)):
        for c in range(count):
            loads.append(
                pltpu.make_async_copy(
                    ref.at[:, pl.ds(c * chunk, chunk)], flat.at[w, c], load_sem.at[w, c]
                )
            )
    prompt_loads = [
        pltpu.make_async_copy(
            prompt_ref.at[:, pl.ds(c * chunk, chunk)], prompt.at[c], prompt_sem.at[c]
        )
        for c in range(count)
    ]
    for copy in loads + prompt_loads:
        copy.start()

    barrier = pltpu.get_barrier_semaphore()
    for to in far:
        pl.semaphore_signal(barrier, inc=1, device_id=(to, f), device_id_type=MESH)
    for to in beside:
        pl.semaphore_signal(barrier, inc=1, device_id=(a, to), device_id_type=MESH)

    def over_adapter(source, target, sems, r, to):
        return pltpu.make_async_remote_copy(
            src_ref=source,
            dst_ref=target,
            send_sem=sems.at[0, r],
            recv_sem=sems.at[1, r],
            device_id=(to, f),
            device_id_type=MESH,
        )

    def over_feature(source, target, sems, r, to):
        return pltpu.make_async_remote_copy(
            src_ref=source,
            dst_ref=target,
            send_sem=sems.at[0, r],
            recv_sem=sems.at[1, r],
            device_id=(a, to),
            device_id_type=MESH,
        )

    for w, ref in enumerate((init_v_ref, init_u_ref)):
        total = jnp.zeros((width, rows), jnp.float32)
        for c in range(count):
            loads[w * count + c].wait()
            basis = ref[:, c * chunk : (c + 1) * chunk].astype(jnp.bfloat16)
            total += dot_nt(basis, flat[w, c])
        init_out[w] = total.astype(init_out.dtype)
    pl.semaphore_wait(barrier, na - 1 + nf - 1)
    copies = [
        over_feature(init_out, init_in.at[r], init_sem, r, to) for r, to in enumerate(beside)
    ]
    for copy in copies:
        copy.start()
    for copy in copies:
        copy.wait()
    total = init_out[...].astype(jnp.float32)
    for r in range(nf - 1):
        total += init_in[r].astype(jnp.float32)
    factors[...] = total

    weights = jnp.zeros((1, rows), jnp.float32)
    lane = lax.broadcasted_iota(jnp.int32, (1, rows), 1) // rank
    for i in range(rows // rank):
        weights = jnp.where(lane == i, weights_ref[i], weights)

    slots = [(r, q) for q in range(na // count) for r in near(count) if r or q]

    def to_device(r, q):
        return lax.rem(lax.rem(base + q * count, na) + lax.rem(mine + r, count), na)

    def half(h, last):
        w = 1 - lax.rem(h, 2)
        parity = 1 - w
        low = weigh(rank, factors[1 - w], factors[w], weights)
        scatter = [[] for _ in range(subs)]
        for r in near(count):
            c = lax.rem(mine + r, count)
            piece = jnp.dot(low, flat[w, c], preferred_element_type=jnp.float32).astype(part.dtype)
            for s in range(subs):
                part[c, s] = piece[:, s * sub : (s + 1) * sub]
            for q in range(na // count):
                if r or q:
                    at = q * count + r - 1
                    for s in range(subs):
                        copy = over_adapter(
                            part.at[c, s],
                            arrived.at[at, s],
                            scatter_sem.at[s],
                            at,
                            to_device(r, q),
                        )
                        scatter[s].append((at, copy))
                        if s == 0:
                            copy.start()
        for s in range(1, subs):
            for _, copy in scatter[s]:
                copy.start()
        if last:
            for c in range(count):
                for s in range(subs):
                    at = c * chunk + s * sub
                    basis_ref[:, at : at + sub] = dot_split(
                        inverse_ref[...], numerator[0, c, s].astype(jnp.float32)
                    ).astype(basis_ref.dtype)
            for copy in prompt_loads:
                copy.wait()
        gather = [[] for _ in range(subs)]
        proj = jnp.zeros((width, rows), jnp.float32)
        gram = jnp.zeros((width, width), jnp.float32)
        hidden = jnp.zeros(hidden_out.shape, jnp.float32) if last else None

        def add(c, s, piece, proj, gram, hidden):
            lanes = slice(s * sub, (s + 1) * sub)
            gram += dot_nt(piece, piece)
            proj += dot_nt(piece, flat[w, c, :, lanes])
            if last:
                hidden += dot_nt(piece, prompt[c, :, lanes])
            return proj, gram, hidden

        for s in range(subs):
            total = part[mine, s].astype(jnp.float32)
            for at, copy in scatter[s]:
                copy.wait_recv()
                total += arrived[at, s].astype(jnp.float32)
            own = total.astype(numerator.dtype)
            numerator[parity, mine, s] = own
            for r in near(count)[1:]:
                copy = over_adapter(
                    numerator.at[parity, mine, s],
                    numerator.at[parity, mine, s],
                    gather_sem.at[s],
                    r - 1,
                    base + lax.rem(mine + r, count),
                )
                copy.start()
                gather[s].append((r, copy))
            proj, gram, hidden = add(mine, s, own, proj, gram, hidden)
        for s in range(subs):
            for r, copy in gather[s]:
                copy.wait_recv()
                c = lax.rem(mine + count - r, count)
                proj, gram, hidden = add(c, s, numerator[parity, c, s], proj, gram, hidden)
        gram_out[...] = fold(gram)
        gram_sends = [
            over_feature(gram_out, gram_in.at[parity, r], gram_sem.at[parity], r, to)
            for r, to in enumerate(beside)
        ]
        for copy in gram_sends:
            copy.start()
        proj_out[...] = proj.astype(proj_out.dtype)
        proj_sends = [
            over_feature(proj_out, proj_in.at[parity, r], proj_sem.at[parity], r, to)
            for r, to in enumerate(beside)
        ]
        for copy in proj_sends:
            copy.start()
        late = []
        if last:
            hidden_out[...] = hidden.astype(hidden_out.dtype)
            late = [
                over_feature(hidden_out, hidden_in.at[r], hidden_sem, r, to)
                for r, to in enumerate(beside)
            ]
            for copy in late:
                copy.start()
            all_q[a] = factors[1].astype(all_q.dtype)
            late += spread(all_q, q_sem)
            for copy in proj_sends:
                copy.wait_recv()
            total = proj_out[...].astype(jnp.float32)
            for r in range(nf - 1):
                total += proj_in[parity, r].astype(jnp.float32)
            all_p[a] = total.astype(all_p.dtype)
            late += spread(all_p, p_sem)
        for copy in gram_sends:
            copy.wait_recv()
        square = gram_out[...]
        for r in range(nf - 1):
            square += gram_in[parity, r]
        inverse = inverse_factor(unfold(square))
        inverse_ref[...] = inverse
        if not last:
            for copy in proj_sends:
                copy.wait_recv()
            total = proj_out[...].astype(jnp.float32)
            for r in range(nf - 1):
                total += proj_in[parity, r].astype(jnp.float32)
            factors[w] = dot32(inverse, total)
        for s in range(subs):
            for _, copy in scatter[s] + gather[s]:
                copy.wait_send()
        for copy in gram_sends + proj_sends:
            copy.wait_send()
        return late

    def spread(table, sems):
        copies = [
            over_adapter(table.at[a], table.at[a], sems, q * count + r - 1, to_device(r, q))
            for r, q in slots
        ]
        for copy in copies:
            copy.start()
        return copies

    def step(h, carry):
        half(h, False)
        return carry

    lax.fori_loop(0, 2 * SWEEPS - 1, step, 0)
    late = half(2 * SWEEPS - 1, True)
    inverse = inverse_ref[...]
    for copy in late[: nf - 1]:
        copy.wait()
    total = hidden_out[...].astype(jnp.float32)
    for r in range(nf - 1):
        total += hidden_in[r].astype(jnp.float32)
    hidden = dot_split(inverse, total).astype(jnp.bfloat16)
    blocks = ids_ref.shape[0]
    block = hidden.shape[1] // blocks
    per = rows // rank
    owners, picks = [], []
    shape = (rows, blocks * rank)
    row, column = lax.broadcasted_iota(jnp.int32, shape, 0), lax.broadcasted_iota(jnp.int32, shape, 1)
    for b in range(blocks):
        at = ids_ref[b]
        owners.append(at // per)
        wanted = (row == column - b * rank + lax.rem(at, per) * rank) & (column // rank == b)
        picks.append(jnp.where(wanted, 1.0, 0.0).astype(jnp.bfloat16))

    def pick(table):
        return sum(
            jnp.dot(table[owners[b]], picks[b], preferred_element_type=jnp.float32)
            for b in range(blocks)
        )

    for copy in late[nf - 1 : nf - 1 + na - 1]:
        copy.wait()
    chosen_q = pick(all_q).astype(jnp.bfloat16)
    for copy in late[nf - 1 + na - 1 :]:
        copy.wait()
    chosen_p = dot32(inverse, pick(all_p)).astype(jnp.bfloat16)
    owner = lax.broadcasted_iota(jnp.int32, (1, blocks * rank), 1) // rank
    for b in range(blocks):
        core = dot_nt(jnp.where(owner == b, chosen_q, 0), chosen_p).astype(jnp.bfloat16)
        mixed = jnp.dot(
            core, hidden[:, b * block : (b + 1) * block], preferred_element_type=jnp.float32
        )
        mixed_ref[b * block : (b + 1) * block, :] = mixed.T.astype(mixed_ref.dtype)


def near(count):
    return sorted(range(count), key=lambda r: (min(r, count - r), r))


def on_device(na, nf, adapter_down, adapter_up, fisher, init_v, init_u, prompt_rows, request_ids):
    count_local, rank, depth = adapter_up.shape
    width = init_v.shape[1]
    rows = count_local * rank
    down = adapter_down.reshape(rows, depth)
    up = adapter_up.reshape(rows, depth)
    tall = prompt_rows.shape[0]
    count = math.gcd(na, depth // LANES)
    chunk = depth // count
    subs = SUBS if chunk % (SUBS * LANES) == 0 else 1
    sub = chunk // subs
    dma = pltpu.SemaphoreType.DMA
    anywhere = pl.BlockSpec(memory_space=pl.ANY)
    vmem = pl.BlockSpec(memory_space=pltpu.VMEM)
    mixed, basis_u = pl.pallas_call(
        functools.partial(kernel, na, nf, rank),
        out_shape=[
            jax.ShapeDtypeStruct((tall, width), jnp.bfloat16),
            jax.ShapeDtypeStruct((width, depth), jnp.bfloat16),
        ],
        in_specs=[anywhere] * 3 + [vmem] * 2 + [pl.BlockSpec(memory_space=pltpu.SMEM)] * 2,
        out_specs=[vmem, vmem],
        scratch_shapes=[
            pltpu.VMEM((2, count, rows, chunk), jnp.bfloat16),
            pltpu.VMEM((count, tall, chunk), jnp.bfloat16),
            pltpu.VMEM((2, width, rows), jnp.float32),
            pltpu.VMEM((count, subs, width, sub), SEND),
            pltpu.VMEM((na - 1, subs, width, sub), SEND),
            pltpu.VMEM((2, count, subs, width, sub), jnp.bfloat16),
            pltpu.VMEM((width, rows), SEND),
            pltpu.VMEM((width // 2, 2 * width), jnp.float32),
            pltpu.VMEM((2, nf - 1, width, rows), SEND),
            pltpu.VMEM((2, nf - 1, width // 2, 2 * width), jnp.float32),
            pltpu.VMEM((2, width, rows), SEND),
            pltpu.VMEM((nf - 1, 2, width, rows), SEND),
            pltpu.VMEM((width, tall), SEND),
            pltpu.VMEM((nf - 1, width, tall), SEND),
            pltpu.VMEM((na, width, rows), jnp.bfloat16),
            pltpu.VMEM((na, width, rows), jnp.bfloat16),
            pltpu.VMEM((width, width), jnp.float32),
            dma((2, count)),
            dma((count,)),
            dma((subs, 2, na - 1)),
            dma((subs, 2, count - 1)),
            dma((2, 2, nf - 1)),
            dma((2, 2, nf - 1)),
            dma((2, nf - 1)),
            dma((2, nf - 1)),
            dma((2, na - 1)),
            dma((2, na - 1)),
        ],
        compiler_params=pltpu.CompilerParams(
            vmem_limit_bytes=63 * 2**20, collective_id=0, has_side_effects=True
        ),
    )(down, up, prompt_rows, init_v.T, init_u.T, fisher, request_ids)
    served = jnp.dot(mixed, basis_u, preferred_element_type=jnp.float32)
    return served.astype(jnp.bfloat16)


def solution(mesh):
    placed = (
        P("adapter", None, "feature"),
        P("adapter", None, "feature"),
        P("adapter"),
        P("feature", None),
        P("feature", None),
        P("adapter", "feature"),
        P("adapter"),
    )
    body = functools.partial(on_device, mesh.shape["adapter"], mesh.shape["feature"])
    return jax.shard_map(
        body, mesh=mesh, in_specs=placed, out_specs=P("adapter", "feature"), check_vma=False
    )
```

time: 178 us -> 145 us (0.81)
  Pallas kernels: 171 us -> 142 us
  local copies, waits for them, and re-layouts: 4.87 us -> 0 us
    pallas_call x1, Pallas kernels: 171 us -> 142 us  [on_device(): pl.pallas_call(functools.partial(kernel, na, nf, rank), out_shape=[jax.Sh...]
    unnamed x8 -> x0, local copies, waits for them, and re-layouts: 3.97 us -> none
where the time goes in v2:
time: 145 us
  Pallas kernels  142 us (98%)
  matrix products  3.03 us (2%)
    pallas_call x1, Pallas kernels, on_device(): pl.pallas_call(functools.partial(kernel, na, nf, rank), out_shape=[jax.Sh...  142 us
    dot_general x1, matrix products, on_device(): served = jnp.dot(mixed, basis_u, preferred_element_type=jnp.float32)  3.03 us

profile of v2, /device:TPU:0, one launch (start us, length us, event | category | flops | bytes accessed | tf_op | source)
XLA Modules:
  0.0 144.9 jit_solution(6678639653102546212)
XLA Ops:
  0.0 141.8 %shard_map.73 = (bf16[512,64]{1,0:T(8,128)(2,1)}, bf16[64,2048]{1,0:T(8,128)(2,1)}) custom-call(bf16[256,2048]{1,0:T(8,128)(2,1)} %bitcast.6, bf16[256,2048]{1,0:T(8,128)(2,1)} %bitcast.7, bf16[512,2048]{1,0:T(8,128)(2,1)} %prompt_ref.1, f32[64,2048]{1,0:T(8,128)} %bitcast.8, f32[64,2048]{1,0:T(8,128)} %bitcast.9, f32[16]{0:T(128)} %weights_ref.1, s32[4]{0:T(128)} %ids_ref.1), custom_call_target="tpu_custom_call" | custom-call | tf_op jit(solution)/shard_map/pallas_call | solution.py:424
  141.8 3.0 %convolution_convert_fusion = bf16[512,2048]{1,0:T(8,128)(2,1)} fusion(bf16[512,64]{1,0:T(8,128)(2,1)} %get-tuple-element.7, bf16[64,2048]{1,0:T(8,128)(2,1)} %get-tuple-element.8), kind=kOutput, calls=%fused_computation | convolution fusion | flops 135266304 | bytes 2424832 | tf_op jit(solution)/shard_map/dot_general | solution.py:465

commit v3 on v2

--- a/solution.py
+++ b/solution.py
@@ -11,16 +11,10 @@
 SWEEPS = 3
 GROUP = 8
 LANES = 128
+VMEM_BYTES = int(53.1 * 2**20)
 MESH = pl.DeviceIdType.MESH
 SUBS = 2
 SEND = jnp.bfloat16
-
-highest = lax.Precision.HIGHEST
-
-
-def dot32(left, right):
-    return jnp.dot(left, right, precision=highest, preferred_element_type=jnp.float32)
-
 
 def dot_nt(left, right):
     return lax.dot_general(
@@ -29,9 +23,8 @@
 
 
 def dot_split(left, right):
-    left_high, right_high = left.astype(jnp.bfloat16), right.astype(jnp.bfloat16)
-    left_low = (left - left_high.astype(jnp.float32)).astype(jnp.bfloat16)
-    right_low = (right - right_high.astype(jnp.float32)).astype(jnp.bfloat16)
+    left_high, left_low = halves(left)
+    right_high, right_low = halves(right)
     dot = functools.partial(jnp.dot, preferred_element_type=jnp.float32)
     return dot(left_high, right_high) + (dot(left_high, right_low) + dot(left_low, right_high))
 
@@ -74,6 +67,11 @@
     return jnp.concatenate(result, axis=0)[:, width:]
 
 
+def halves(full):
+    high = full.astype(jnp.bfloat16)
+    return high, (full - high.astype(jnp.float32)).astype(jnp.bfloat16)
+
+
 def weigh(rank, fresh, other, weights):
     total = fresh.shape[1]
     step = 128 if total % 128 == 0 and 128 % rank == 0 else total
@@ -81,11 +79,25 @@
         lax.broadcasted_iota(jnp.int32, (step, step), 0) // rank
         == lax.broadcasted_iota(jnp.int32, (step, step), 1) // rank
     )
+    dot = functools.partial(jnp.dot, preferred_element_type=jnp.float32)
     parts = []
     for at in range(0, total, step):
-        piece = fresh[:, at : at + step]
-        inner = jnp.where(same, dot_split(piece.T, piece), 0.0)
-        parts.append(dot_split(other[:, at : at + step], inner))
+        high, low = halves(fresh[:, at : at + step])
+        inner = lax.dot_general(
+            jnp.concatenate([high, high, low], axis=0),
+            jnp.concatenate([high, low, high], axis=0),
+            (((0,), (0,)), ((), ())),
+            preferred_element_type=jnp.float32,
+        )
+        inner_high, inner_low = halves(jnp.where(same, inner, 0.0))
+        other_high, other_low = halves(other[:, at : at + step])
+        parts.append(
+            dot(
+                jnp.concatenate([other_high, other_high], axis=1),
+                jnp.concatenate([inner_high, inner_low], axis=0),
+            )
+            + dot(other_low, inner_high)
+        )
     joined = parts[0] if len(parts) == 1 else jnp.concatenate(parts, axis=1)
     return (joined * weights).astype(jnp.bfloat16)
 
@@ -127,11 +139,18 @@
     init_in,
     hidden_out,
     hidden_in,
-    all_q,
-    all_p,
+    starts,
+    asked,
+    picks,
+    q_out,
+    q_in,
+    p_out,
+    p_in,
     inverse_ref,
+    start_sem,
     load_sem,
     prompt_sem,
+    asked_sem,
     scatter_sem,
     gather_sem,
     proj_sem,
@@ -151,21 +170,24 @@
     beside = [lax.rem(f + r, nf) for r in range(1, nf)]
 
     loads = []
-    for w, ref in enumerate((down_ref, up_ref)):
-        for c in range(count):
-            loads.append(
+    for w, (start_ref, ref) in enumerate(((init_v_ref, down_ref), (init_u_ref, up_ref))):
+        loads.append(
+            [pltpu.make_async_copy(start_ref, starts.at[w], start_sem.at[w])]
+            + [
                 pltpu.make_async_copy(
                     ref.at[:, pl.ds(c * chunk, chunk)], flat.at[w, c], load_sem.at[w, c]
                 )
-            )
+                for c in range(count)
+            ]
+        )
+        for copy in loads[w]:
+            copy.start()
     prompt_loads = [
         pltpu.make_async_copy(
             prompt_ref.at[:, pl.ds(c * chunk, chunk)], prompt.at[c], prompt_sem.at[c]
         )
         for c in range(count)
     ]
-    for copy in loads + prompt_loads:
-        copy.start()
 
     barrier = pltpu.get_barrier_semaphore()
     for to in far:
@@ -193,20 +215,47 @@
             device_id_type=MESH,
         )
 
-    for w, ref in enumerate((init_v_ref, init_u_ref)):
+    slots = [(r, q) for q in range(na // count) for r in offsets(count) if r or q]
+
+    def slot_of(r, q):
+        return q * count + r - 1
+
+    def to_device(r, q):
+        return lax.rem(lax.rem(base + q * count, na) + lax.rem(mine + r, count), na)
+
+    blocks = ids_ref.shape[0]
+    wide = blocks * rank
+    column = lax.broadcasted_iota(jnp.int32, asked.shape[1:], 1) // rank
+    wanted = jnp.zeros(asked.shape[1:], jnp.int32)
+    for i in range(blocks):
+        wanted = jnp.where(column == i, ids_ref[i], wanted)
+    asked[a] = wanted
+
+    first_sends = []
+    for w in range(2):
         total = jnp.zeros((width, rows), jnp.float32)
+        loads[w][0].wait()
         for c in range(count):
-            loads[w * count + c].wait()
-            basis = ref[:, c * chunk : (c + 1) * chunk].astype(jnp.bfloat16)
+            loads[w][1 + c].wait()
+            basis = starts[w, :, c * chunk : (c + 1) * chunk].astype(jnp.bfloat16)
             total += dot_nt(basis, flat[w, c])
         init_out[w] = total.astype(init_out.dtype)
-    pl.semaphore_wait(barrier, na - 1 + nf - 1)
-    copies = [
-        over_feature(init_out, init_in.at[r], init_sem, r, to) for r, to in enumerate(beside)
+        if w == 0:
+            pl.semaphore_wait(barrier, na - 1 + nf - 1)
+        copies = [
+            over_feature(init_out.at[w], init_in.at[r, w], init_sem.at[w], r, to)
+            for r, to in enumerate(beside)
+        ]
+        for copy in copies:
+            copy.start()
+        first_sends += copies
+    asked_sends = [
+        over_adapter(asked.at[a], asked.at[a], asked_sem, slot_of(r, q), to_device(r, q))
+        for r, q in slots
     ]
-    for copy in copies:
+    for copy in asked_sends + prompt_loads:
         copy.start()
-    for copy in copies:
+    for copy in first_sends:
         copy.wait()
     total = init_out[...].astype(jnp.float32)
     for r in range(nf - 1):
@@ -218,24 +267,19 @@
     for i in range(rows // rank):
         weights = jnp.where(lane == i, weights_ref[i], weights)
 
-    slots = [(r, q) for q in range(na // count) for r in near(count) if r or q]
-
-    def to_device(r, q):
-        return lax.rem(lax.rem(base + q * count, na) + lax.rem(mine + r, count), na)
-
     def half(h, last):
         w = 1 - lax.rem(h, 2)
         parity = 1 - w
         low = weigh(rank, factors[1 - w], factors[w], weights)
         scatter = [[] for _ in range(subs)]
-        for r in near(count):
+        for r in offsets(count):
             c = lax.rem(mine + r, count)
             piece = jnp.dot(low, flat[w, c], preferred_element_type=jnp.float32).astype(part.dtype)
             for s in range(subs):
                 part[c, s] = piece[:, s * sub : (s + 1) * sub]
             for q in range(na // count):
                 if r or q:
-                    at = q * count + r - 1
+                    at = slot_of(r, q)
                     for s in range(subs):
                         copy = over_adapter(
                             part.at[c, s],
@@ -257,20 +301,19 @@
                     basis_ref[:, at : at + sub] = dot_split(
                         inverse_ref[...], numerator[0, c, s].astype(jnp.float32)
                     ).astype(basis_ref.dtype)
+            choose()
+            late = spread(factors[1], q_out, q_in, q_sem)
             for copy in prompt_loads:
                 copy.wait()
         gather = [[] for _ in range(subs)]
         proj = jnp.zeros((width, rows), jnp.float32)
         gram = jnp.zeros((width, width), jnp.float32)
-        hidden = jnp.zeros(hidden_out.shape, jnp.float32) if last else None
-
-        def add(c, s, piece, proj, gram, hidden):
+
+        def add(c, s, piece, proj, gram):
             lanes = slice(s * sub, (s + 1) * sub)
             gram += dot_nt(piece, piece)
             proj += dot_nt(piece, flat[w, c, :, lanes])
-            if last:
-                hidden += dot_nt(piece, prompt[c, :, lanes])
-            return proj, gram, hidden
+            return proj, gram
 
         for s in range(subs):
             total = part[mine, s].astype(jnp.float32)
@@ -279,7 +322,7 @@
                 total += arrived[at, s].astype(jnp.float32)
             own = total.astype(numerator.dtype)
             numerator[parity, mine, s] = own
-            for r in near(count)[1:]:
+            for r in offsets(count)[1:]:
                 copy = over_adapter(
                     numerator.at[parity, mine, s],
                     numerator.at[parity, mine, s],
@@ -289,12 +332,12 @@
                 )
                 copy.start()
                 gather[s].append((r, copy))
-            proj, gram, hidden = add(mine, s, own, proj, gram, hidden)
+            proj, gram = add(mine, s, own, proj, gram)
         for s in range(subs):
             for r, copy in gather[s]:
                 copy.wait_recv()
                 c = lax.rem(mine + count - r, count)
-                proj, gram, hidden = add(c, s, numerator[parity, c, s], proj, gram, hidden)
+                proj, gram = add(c, s, numerator[parity, c, s], proj, gram)
         gram_out[...] = fold(gram)
         gram_sends = [
             over_feature(gram_out, gram_in.at[parity, r], gram_sem.at[parity], r, to)
@@ -309,24 +352,25 @@
         ]
         for copy in proj_sends:
             copy.start()
-        late = []
         if last:
+            hidden = jnp.zeros(hidden_out.shape, jnp.float32)
+            for c in range(count):
+                for s in range(subs):
+                    lanes = slice(s * sub, (s + 1) * sub)
+                    hidden += dot_nt(numerator[parity, c, s], prompt[c, :, lanes])
             hidden_out[...] = hidden.astype(hidden_out.dtype)
-            late = [
+            hidden_sends = [
                 over_feature(hidden_out, hidden_in.at[r], hidden_sem, r, to)
                 for r, to in enumerate(beside)
             ]
-            for copy in late:
+            for copy in hidden_sends:
                 copy.start()
-            all_q[a] = factors[1].astype(all_q.dtype)
-            late += spread(all_q, q_sem)
             for copy in proj_sends:
                 copy.wait_recv()
             total = proj_out[...].astype(jnp.float32)
             for r in range(nf - 1):
                 total += proj_in[parity, r].astype(jnp.float32)
-            all_p[a] = total.astype(all_p.dtype)
-            late += spread(all_p, p_sem)
+            late = hidden_sends + late + spread(total, p_out, p_in, p_sem)
         for copy in gram_sends:
             copy.wait_recv()
         square = gram_out[...]
@@ -340,22 +384,42 @@
             total = proj_out[...].astype(jnp.float32)
             for r in range(nf - 1):
                 total += proj_in[parity, r].astype(jnp.float32)
-            factors[w] = dot32(inverse, total)
+            factors[w] = dot_split(inverse, total)
         for s in range(subs):
             for _, copy in scatter[s] + gather[s]:
                 copy.wait_send()
         for copy in gram_sends + proj_sends:
             copy.wait_send()
-        return late
-
-    def spread(table, sems):
-        copies = [
-            over_adapter(table.at[a], table.at[a], sems, q * count + r - 1, to_device(r, q))
-            for r, q in slots
-        ]
-        for copy in copies:
-            copy.start()
+        return late if last else None
+
+    def choose():
+        for copy in asked_sends:
+            copy.wait()
+        shape = (rows, wide)
+        row = lax.broadcasted_iota(jnp.int32, shape, 0)
+        inside = lax.rem(row, rank) == lax.rem(lax.broadcasted_iota(jnp.int32, shape, 1), rank)
+        number = a * (rows // rank) + row // rank
+        for r, q in [(0, 0)] + slots:
+            hit = inside & (number == asked[to_device(r, q), :1, :wide])
+            picks[slot_of(r, q) + 1] = jnp.where(hit, 1.0, 0.0).astype(picks.dtype)
+
+    def spread(table, out, into, sems):
+        low = table.astype(jnp.bfloat16)
+        copies = []
+        for r, q in slots + [(0, 0)]:
+            at = slot_of(r, q)
+            piece = jnp.dot(low, picks[at + 1], preferred_element_type=jnp.float32)
+            out[at + 1] = fold(piece).astype(out.dtype)
+            if r or q:
+                copies.append(over_adapter(out.at[at + 1], into.at[at], sems, at, to_device(r, q)))
+                copies[-1].start()
         return copies
+
+    def gathered(out, into):
+        total = out[0].astype(jnp.float32)
+        for r in range(na - 1):
+            total += into[r].astype(jnp.float32)
+        return unfold(total)
 
     def step(h, carry):
         half(h, False)
@@ -369,42 +433,23 @@
     total = hidden_out[...].astype(jnp.float32)
     for r in range(nf - 1):
         total += hidden_in[r].astype(jnp.float32)
-    hidden = dot_split(inverse, total).astype(jnp.bfloat16)
-    blocks = ids_ref.shape[0]
-    block = hidden.shape[1] // blocks
-    per = rows // rank
-    owners, picks = [], []
-    shape = (rows, blocks * rank)
-    row, column = lax.broadcasted_iota(jnp.int32, shape, 0), lax.broadcasted_iota(jnp.int32, shape, 1)
-    for b in range(blocks):
-        at = ids_ref[b]
-        owners.append(at // per)
-        wanted = (row == column - b * rank + lax.rem(at, per) * rank) & (column // rank == b)
-        picks.append(jnp.where(wanted, 1.0, 0.0).astype(jnp.bfloat16))
-
-    def pick(table):
-        return sum(
-            jnp.dot(table[owners[b]], picks[b], preferred_element_type=jnp.float32)
-            for b in range(blocks)
-        )
-
+    hidden = dot_split(inverse, total).T.astype(jnp.bfloat16)
     for copy in late[nf - 1 : nf - 1 + na - 1]:
         copy.wait()
-    chosen_q = pick(all_q).astype(jnp.bfloat16)
+    chosen_q = gathered(q_out, q_in).astype(jnp.bfloat16)
+    owner = lax.broadcasted_iota(jnp.int32, (1, wide), 1) // rank
     for copy in late[nf - 1 + na - 1 :]:
         copy.wait()
-    chosen_p = dot32(inverse, pick(all_p)).astype(jnp.bfloat16)
-    owner = lax.broadcasted_iota(jnp.int32, (1, blocks * rank), 1) // rank
-    for b in range(blocks):
-        core = dot_nt(jnp.where(owner == b, chosen_q, 0), chosen_p).astype(jnp.bfloat16)
-        mixed = jnp.dot(
-            core, hidden[:, b * block : (b + 1) * block], preferred_element_type=jnp.float32
-        )
-        mixed_ref[b * block : (b + 1) * block, :] = mixed.T.astype(mixed_ref.dtype)
-
-
-def near(count):
-    return sorted(range(count), key=lambda r: (min(r, count - r), r))
+    chosen_p = dot_split(inverse, gathered(p_out, p_in)).astype(jnp.bfloat16)
+    block = hidden.shape[0] // blocks
+    for i in range(blocks):
+        core = dot_nt(jnp.where(owner == i, chosen_q, 0), chosen_p).astype(jnp.bfloat16)
+        lines = slice(i * block, (i + 1) * block)
+        mixed_ref[lines, :] = dot_nt(hidden[lines], core).astype(mixed_ref.dtype)
+
+
+def offsets(count):
+    return [0] + sorted(range(1, count), key=lambda r: (-min(r, count - r), r))
 
 
 def on_device(na, nf, adapter_down, adapter_up, fisher, init_v, init_u, prompt_rows, request_ids):
@@ -413,7 +458,7 @@
     rows = count_local * rank
     down = adapter_down.reshape(rows, depth)
     up = adapter_up.reshape(rows, depth)
-    tall = prompt_rows.shape[0]
+    tall, blocks = prompt_rows.shape[0], request_ids.shape[0]
     count = math.gcd(na, depth // LANES)
     chunk = depth // count
     subs = SUBS if chunk % (SUBS * LANES) == 0 else 1
@@ -427,7 +472,7 @@
             jax.ShapeDtypeStruct((tall, width), jnp.bfloat16),
             jax.ShapeDtypeStruct((width, depth), jnp.bfloat16),
         ],
-        in_specs=[anywhere] * 3 + [vmem] * 2 + [pl.BlockSpec(memory_space=pltpu.SMEM)] * 2,
+        in_specs=[anywhere] * 5 + [pl.BlockSpec(memory_space=pltpu.SMEM)] * 2,
         out_specs=[vmem, vmem],
         scratch_shapes=[
             pltpu.VMEM((2, count, rows, chunk), jnp.bfloat16),
@@ -444,22 +489,29 @@
             pltpu.VMEM((nf - 1, 2, width, rows), SEND),
             pltpu.VMEM((width, tall), SEND),
             pltpu.VMEM((nf - 1, width, tall), SEND),
-            pltpu.VMEM((na, width, rows), jnp.bfloat16),
-            pltpu.VMEM((na, width, rows), jnp.bfloat16),
+            pltpu.VMEM((2, width, depth), jnp.float32),
+            pltpu.VMEM((na, 8, -(-blocks * rank // LANES) * LANES), jnp.int32),
+            pltpu.VMEM((na, rows, blocks * rank), jnp.bfloat16),
+            pltpu.VMEM((na, width // 2, 2 * blocks * rank), jnp.bfloat16),
+            pltpu.VMEM((na - 1, width // 2, 2 * blocks * rank), jnp.bfloat16),
+            pltpu.VMEM((na, width // 2, 2 * blocks * rank), jnp.bfloat16),
+            pltpu.VMEM((na - 1, width // 2, 2 * blocks * rank), jnp.bfloat16),
             pltpu.VMEM((width, width), jnp.float32),
+            dma((2,)),
             dma((2, count)),
             dma((count,)),
+            dma((2, na - 1)),
             dma((subs, 2, na - 1)),
             dma((subs, 2, count - 1)),
             dma((2, 2, nf - 1)),
             dma((2, 2, nf - 1)),
-            dma((2, nf - 1)),
+            dma((2, 2, nf - 1)),
             dma((2, nf - 1)),
             dma((2, na - 1)),
             dma((2, na - 1)),
         ],
         compiler_params=pltpu.CompilerParams(
-            vmem_limit_bytes=63 * 2**20, collective_id=0, has_side_effects=True
+            vmem_limit_bytes=VMEM_BYTES, collective_id=0, has_side_effects=True
         ),
     )(down, up, prompt_rows, init_v.T, init_u.T, fisher, request_ids)
     served = jnp.dot(mixed, basis_u, preferred_element_type=jnp.float32)

time: 145 us -> 141 us (0.972)
  Pallas kernels: 142 us -> 137 us
    pallas_call x1, Pallas kernels: 142 us -> 137 us  [on_device(): pl.pallas_call(functools.partial(kernel, na, nf, rank), out_shape=[jax.Sh...]
where the time goes in v3:
time: 141 us
  Pallas kernels  137 us (97%)
  matrix products  2 us (1%)
    pallas_call x1, Pallas kernels, on_device(): pl.pallas_call(functools.partial(kernel, na, nf, rank), out_shape=[jax.Sh...  137 us

profile of v3, /device:TPU:0, one launch (start us, length us, event | category | flops | bytes accessed | tf_op | source)
XLA Modules:
  0.0 140.5 jit_solution(9696765287550254526)
XLA Ops:
  0.0 0.0 copy-start
  0.0 0.7 copy-done
  0.7 0.0 copy-start.1
  0.7 0.7 copy-done.1
  1.3 137.2 %shard_map.73 = (bf16[512,64]{1,0:T(8,128)(2,1)S(1)}, bf16[64,2048]{1,0:T(8,128)(2,1)S(1)}) custom-call(bf16[256,2048]{1,0:T(8,128)(2,1)} %bitcast.6, bf16[256,2048]{1,0:T(8,128)(2,1)} %bitcast.7, bf16[512,2048]{1,0:T(8,128)(2,1)} %prompt_ref.1, f32[64,2048]{1,0:T(8,128)} %bitcast.8, f32[64,2048]{1,0:T(8,128)} %bitcast.9, f32[16]{0:T(128)S(1)} %copy-done, ...), custom_call_target="tpu_custom_call" | custom-call | tf_op jit(solution)/shard_map/pallas_call | solution.py:469
  138.5 2.0 %convolution_convert_fusion = bf16[512,2048]{1,0:T(8,128)(2,1)} fusion(bf16[512,64]{1,0:T(8,128)(2,1)S(1)} %get-tuple-element.7, bf16[64,2048]{1,0:T(8,128)(2,1)S(1)} %get-tuple-element.8), kind=kOutput, calls=%fused_computation | convolution fusion | flops 135266304 | bytes 2424832 | tf_op jit(solution)/shard_map/dot_general | solution.py:517
Async XLA Ops:
  0.0 0.7 copy-start
  0.7 0.7 copy-start.1
